TPU v7x, 128 devices: a whole 4x4x4 slice. The times are simulated.
128 devices in a mesh: mp: 8 (over x, z_lo), item: 16 (over z_hi, y, core).
Axes of the slice: x: 4, y: 4, z: 4 (z_hi: 2, z_lo: 2; z = z_hi * 2 + z_lo), core: 2. Of those that a mesh axis runs over, the one named last changes fastest.
Arguments:
- response: int32 [16384, 32768], P('mp', 'item'), may hold values from 0 to 2
- difficulty: float32 [32768], P('item'), may hold values from -4 to 4
- ability: float32 [16384, 256], P('mp', 'item'), may hold values from -6 to 6
- ability_m: float32 [16384, 256], P('mp', 'item'), may hold values from -3 to 3
- ability_v: float32 [16384, 256], P('mp', 'item'), may hold values from 0.02 to 0.5
- discrim: float32 [32768, 256], P('item', 'mp'), may hold values from -0.375 to 0.375
- discrim_m: float32 [32768, 256], P('item', 'mp'), may hold values from -3 to 3
- discrim_v: float32 [32768, 256], P('item', 'mp'), may hold values from 0.02 to 0.5
Outputs:
- ability_new: float32 [16384, 256], P('mp', 'item')
- ability_m_new: float32 [16384, 256], P('mp', 'item')
- ability_v_new: float32 [16384, 256], P('mp', 'item')
- discrim_new: float32 [32768, 256], P('item', 'mp')
- discrim_m_new: float32 [32768, 256], P('item', 'mp')
- discrim_v_new: float32 [32768, 256], P('item', 'mp')
Inputs may be any that keep to these rules, and one draw needn't show every extreme that they name: `response`: 0 marks an unobserved pair, 1 an observed wrong answer, 2 an observed right answer.
All inputs are finite; a program needn't handle non-finite values.
Results may differ from a plain program's by a relative error of at most 0.0012.
Values may be sent and summed in bfloat16 or wider, within the bound.
A program may use at most 128 MiB of HBM per device.

v0:
```python
import math
import jax
import jax.numpy as jnp
from jax import lax
from jax.sharding import PartitionSpec as P

K = 256
beta_one = 0.9
beta_two = 0.999
corr_one = 1.0 - 0.9**10
corr_two = 1.0 - 0.999**10
adam_eps = 1e-08


def adam_update(factor, moment, second, gradient, step_rate):
    moment_new = beta_one * moment + (1.0 - beta_one) * gradient
    second_new = beta_two * second + (1.0 - beta_two) * gradient * gradient
    update = moment_new / corr_one / (jnp.sqrt(second_new / corr_two) + adam_eps)
    return (factor - step_rate * update, moment_new, second_new)


def shards(response, difficulty, ability, ability_m, ability_v, discrim, discrim_m, discrim_v):
    ability_full = lax.all_gather(ability.astype(jnp.bfloat16), "item", axis=1, tiled=True)
    discrim_full = lax.all_gather(discrim.astype(jnp.bfloat16), "mp", axis=1, tiled=True)
    logits = lax.dot_general(
        ability_full, discrim_full, (((1,), (1,)), ((), ())), preferred_element_type=jnp.float32
    )
    logits = logits + difficulty[None, :]
    correct = (response == 2).astype(jnp.float32)
    residual = jnp.where(response > 0, jax.nn.sigmoid(logits) - correct, jnp.float32(0.0))
    ability_wide = ability_full.astype(jnp.float32)
    discrim_wide = discrim_full.astype(jnp.float32)
    highest = lax.Precision.HIGHEST
    ability_cols = ability.shape[1]
    discrim_cols = discrim.shape[1]
    items_total = response.shape[1] * lax.axis_size("item")
    ckpts_total = response.shape[0] * lax.axis_size("mp")
    ability_partial = jnp.dot(residual, discrim_wide, precision=highest)
    ability_sum = lax.psum(ability_partial, "item")
    ability_grad = lax.dynamic_slice_in_dim(
        ability_sum, lax.axis_index("item") * ability_cols, ability_cols, 1
    )
    discrim_partial = lax.dot_general(
        residual, ability_wide, (((0,), (0,)), ((), ())), precision=highest
    )
    discrim_sum = lax.psum(discrim_partial, "mp")
    discrim_grad = lax.dynamic_slice_in_dim(
        discrim_sum, lax.axis_index("mp") * discrim_cols, discrim_cols, 1
    )
    ability_grad = ability_grad * math.sqrt(K / items_total)
    discrim_grad = discrim_grad * math.sqrt(1.0 / ckpts_total)
    ability_new, ability_m_new, ability_v_new = adam_update(
        ability, ability_m, ability_v, ability_grad, 0.05
    )
    discrim_new, discrim_m_new, discrim_v_new = adam_update(
        discrim, discrim_m, discrim_v, discrim_grad, 0.01
    )
    return (ability_new, ability_m_new, ability_v_new, discrim_new, discrim_m_new, discrim_v_new)


def solution(mesh):
    return jax.shard_map(
        shards,
        mesh=mesh,
        in_specs=(
            P("mp", "item"),
            P("item"),
            P("mp", "item"),
            P("mp", "item"),
            P("mp", "item"),
            P("item", "mp"),
            P("item", "mp"),
            P("item", "mp"),
        ),
        out_specs=(
            P("mp", "item"),
            P("mp", "item"),
            P("mp", "item"),
            P("item", "mp"),
            P("item", "mp"),
            P("item", "mp"),
        ),
        check_vma=False,
    )
```

profile of v0, /device:TPU:8, one launch (start us, length us, event | category | flops | bytes accessed | tf_op | source)
XLA Modules:
  0.0 386.6 jit_solution(2040958627910483739)
XLA Ops:
  7.2 0.0 all-gather.5.cloned.1.call-start
  7.2 1.6 convert_element_type.12
  8.8 0.0 all-gather.5.cloned.1.call-update
  8.9 0.0 all-gather.3.cloned.1.call-start
  8.9 1.5 convert_element_type.11
  10.5 0.0 all-gather.3.cloned.1.call-update
  10.5 0.0 all-reduce.3.cloned.1.call-start
  10.5 40.9 %all-gather.5.cloned.1.call-done = bf16[2048,256]{0,1:T(8,128)(2,1)} async-done(((bf16[2048,32]{0,1:T(8,128)(2,1)}), bf16[2048,256]{0,1:T(8,128)(2,1)}) %all-gather.5.cloned.1.call-update) | async-done | bytes 1048592 | tf_op jit(solution)/shard_map/all_gather | solution.py:24
  51.5 47.4 %all-gather.3.cloned.1.call-done = bf16[2048,256]{0,1:T(8,128)(2,1)} async-done(((bf16[2048,16]{0,1:T(8,128)(2,1)}), bf16[2048,256]{0,1:T(8,128)(2,1)}) %all-gather.3.cloned.1.call-update) | async-done | bytes 1048592 | tf_op jit(solution)/shard_map/all_gather | solution.py:23
  98.8 12.2 %subtract_select_fusion = f32[2048,2048]{1,0:T(8,128)S(1)} fusion(s32[2048,2048]{1,0:T(8,128)} %param.8, bf16[2048,256]{0,1:T(8,128)(2,1)} %all-gather.3.cloned.1.call-done, bf16[2048,256]{0,1:T(8,128)(2,1)} %all-gather.5.cloned.1.call-done, f32[2048]{0:T(1024)} %param.9), kind=kOutput, calls=%fused_computation | convolution fusion | flops 2185232384 | bytes 35659776 | tf_op jit(solution)/shard_map/dot_general | solution.py:25
  111.0 5.7 %copy-done = f32[2048,2048]{1,0:T(8,128)} copy-done((f32[2048,2048]{1,0:T(8,128)}, f32[2048,2048]{1,0:T(8,128)S(1)}, u32[]{:S(2)}) %copy-start) | copy-done | bytes 16777240
  116.7 9.8 %fusion = f32[2048,256]{0,1:T(8,128)} fusion(f32[2048,2048]{1,0:T(8,128)S(1)} %subtract_select_fusion, bf16[2048,256]{0,1:T(8,128)(2,1)S(1)} %copy-done.2), kind=kOutput, calls=%fused_computation.7 | convolution fusion | flops 12884901888 | bytes 19922944 | tf_op jit(solution)/shard_map/dot_general | solution.py:38
  126.5 0.0 copy-start.5
  126.5 0.0 copy-start.6
  126.5 0.0 all-reduce.3.cloned.1.call-update
  126.6 0.2 all-reduce.5.cloned.1.call-start
  126.8 13.3 %fusion.1 = f32[2048,256]{0,1:T(8,128)} fusion(f32[2048,2048]{1,0:T(8,128)} %copy-done, bf16[2048,256]{0,1:T(8,128)(2,1)S(1)} %copy-done.1), kind=kOutput, calls=%fused_computation.8 | convolution fusion | flops 12884901888 | bytes 19922944 | tf_op jit(solution)/shard_map/dot_general | solution.py:43
  140.1 0.0 all-reduce.5.cloned.1.call-update
  140.1 124.7 %all-reduce.3.cloned.1.call-done = f32[2048,256]{0,1:T(8,128)} async-done(((f32[2048,256]{0,1:T(8,128)}), f32[2048,256]{0,1:T(8,128)}) %all-reduce.3.cloned.1.call-update) | async-done | bytes 2097168 | tf_op jit(solution)/shard_map/psum | solution.py:39
  264.8 0.0 copy-done.4
  264.8 0.0 copy-done.8
  264.8 1.7 multiply_subtract_fusion.1
  266.5 111.6 %all-reduce.5.cloned.1.call-done = f32[2048,256]{0,1:T(8,128)} async-done(((f32[2048,256]{0,1:T(8,128)}), f32[2048,256]{0,1:T(8,128)}) %all-reduce.5.cloned.1.call-update) | async-done | bytes 2097168 | tf_op jit(solution)/shard_map/psum | solution.py:46
  378.1 1.9 multiply_subtract_fusion
  (13 shorter events, 0.0 us)
Async XLA Ops:
  7.2 44.3 %all-gather.5.cloned.1.call-start = ((), (), s32[]{:S(2)}) async-start(), calls=%async_computation.1 | async-start | bytes 1179648 | tf_op jit(solution)/shard_map/all_gather | solution.py:24
  8.9 90.0 %all-gather.3.cloned.1.call-start = ((), (), s32[]{:S(2)}) async-start(), calls=%async_computation | async-start | bytes 1114112 | tf_op jit(solution)/shard_map/all_gather | solution.py:23
  10.5 254.3 %all-reduce.3.cloned.1.call-start = ((), (), s32[]{:S(2)}) async-start(), calls=%async_computation.2 | async-start | bytes 4194304 | tf_op jit(solution)/shard_map/psum | solution.py:39
  51.5 65.3 %copy-start.2 = (bf16[2048,256]{0,1:T(8,128)(2,1)S(1)}, bf16[2048,256]{0,1:T(8,128)(2,1)}, u32[]{:S(2)}) copy-start(bf16[2048,256]{0,1:T(8,128)(2,1)} %all-gather.5.cloned.1.call-done) | copy-start | bytes 3145732
  111.0 5.7 %copy-start = (f32[2048,2048]{1,0:T(8,128)}, f32[2048,2048]{1,0:T(8,128)S(1)}, u32[]{:S(2)}) copy-start(f32[2048,2048]{1,0:T(8,128)S(1)} %subtract_select_fusion) | copy-start | bytes 50331652
  116.7 10.1 %copy-start.1 = (bf16[2048,256]{0,1:T(8,128)(2,1)S(1)}, bf16[2048,256]{0,1:T(8,128)(2,1)}, u32[]{:S(2)}) copy-start(bf16[2048,256]{0,1:T(8,128)(2,1)} %all-gather.3.cloned.1.call-done) | copy-start | bytes 3145732
  126.5 138.3 %copy-start.4 = (f32[2048,16]{0,1:T(8,128)S(1)}, f32[2048,16]{0,1:T(8,128)}, u32[]{:S(2)}) copy-start(f32[2048,16]{0,1:T(8,128)} %param.10) | copy-start | bytes 393220
  126.5 138.3 %copy-start.7 = (f32[2048,16]{0,1:T(8,128)S(1)}, f32[2048,16]{0,1:T(8,128)}, u32[]{:S(2)}) copy-start(f32[2048,16]{0,1:T(8,128)} %param.11) | copy-start | bytes 393220
  126.5 138.3 %copy-start.8 = (f32[2048,16]{0,1:T(8,128)S(1)}, f32[2048,16]{0,1:T(8,128)}, u32[]{:S(2)}) copy-start(f32[2048,16]{0,1:T(8,128)} %param.12) | copy-start | bytes 393220
  126.5 251.6 %copy-start.3 = (f32[2048,32]{0,1:T(8,128)S(1)}, f32[2048,32]{0,1:T(8,128)}, u32[]{:S(2)}) copy-start(f32[2048,32]{0,1:T(8,128)} %param.13) | copy-start | bytes 786436
  126.5 251.6 %copy-start.5 = (f32[2048,32]{0,1:T(8,128)S(1)}, f32[2048,32]{0,1:T(8,128)}, u32[]{:S(2)}) copy-start(f32[2048,32]{0,1:T(8,128)} %param.14) | copy-start | bytes 786436
  126.5 251.6 %copy-start.6 = (f32[2048,32]{0,1:T(8,128)S(1)}, f32[2048,32]{0,1:T(8,128)}, u32[]{:S(2)}) copy-start(f32[2048,32]{0,1:T(8,128)} %param.15) | copy-start | bytes 786436
  126.6 251.6 %all-reduce.5.cloned.1.call-start = ((), (), s32[]{:S(2)}) async-start(), calls=%async_computation.3 | async-start | bytes 4194304 | tf_op jit(solution)/shard_map/psum | solution.py:46
Sparse Core Ops, SparseCore 0:
  10.2 41.2 all-gather.4
  54.5 44.3 all-gather.2
  126.7 138.0 all-reduce.2
  267.2 110.9 all-reduce.4
where the time goes:
time: 387 us
  waiting for transfers between devices  325 us (84%)
  matrix products  35.2 us (9%)
  between operations  13.8 us (4%)
  other arithmetic  6.8 us (2%)
  local copies, waits for them, and re-layouts  5.78 us (1%)
    psum x1, waiting for transfers between devices, shards(): ability_sum = lax.psum(ability_partial, 'item')  125 us
    psum x1, waiting for transfers between devices, shards(): discrim_sum = lax.psum(discrim_partial, 'mp')  112 us
    all_gather x1, waiting for transfers between devices, shards(): lax.all_gather(ability.astype(jnp.bfloat16), 'item', axis=1, tiled=True)  47.4 us
    all_gather x1, waiting for transfers between devices, shards(): lax.all_gather(discrim.astype(jnp.bfloat16), 'mp', axis=1, tiled=True)  40.9 us
    dot_general x1, matrix products, shards(): lax.dot_general(residual, ability_wide, (((0,), (0,)), ((), ())), precisi...  13.3 us
    dot_general x1, matrix products, shards(): lax.dot_general(ability_full, discrim_full, (((1,), (1,)), ((), ())), pre...  12.2 us
    dot_general x1, matrix products, shards(): ability_partial = jnp.dot(residual, discrim_wide, precision=highest)  9.76 us
  transfers between devices with their start and end apart: 4, of which 4 were waited for; matrix products, arithmetic and copies ran while one was open for 4% of the time, Pallas kernels for 0%

commit v1 on v0

--- a/solution.py
+++ b/solution.py
@@ -20,7 +20,12 @@
 
 
 def shards(response, difficulty, ability, ability_m, ability_v, discrim, discrim_m, discrim_v):
-    ability_full = lax.all_gather(ability.astype(jnp.bfloat16), "item", axis=1, tiled=True)
+    ability_full = jnp.concatenate(
+        lax.all_to_all(
+            jnp.stack([ability.astype(jnp.bfloat16)] * lax.axis_size("item")), "item", 0, 0
+        ),
+        axis=1,
+    )
     discrim_full = lax.all_gather(discrim.astype(jnp.bfloat16), "mp", axis=1, tiled=True)
     logits = lax.dot_general(
         ability_full, discrim_full, (((1,), (1,)), ((), ())), preferred_element_type=jnp.float32

time: 387 us -> 347 us (0.90)
  waiting for transfers between devices: 325 us -> 260 us
  blocking collectives: 0 us -> 26.3 us
    all_gather x1 -> x0, waiting for transfers between devices: 47.4 us -> none  [shards(): lax.all_gather(ability.astype(jnp.bfloat16), 'item', axis=1, tiled=True)]
    all_to_all x0 -> x1, blocking collectives: none -> 26.3 us  [shards(): lax.all_to_all(jnp.stack([ability.astype(jnp.bfloat16)] * lax.axis_size('...]
    all_gather x1, waiting for transfers between devices: 40.9 us -> 21.6 us  [shards(): lax.all_gather(discrim.astype(jnp.bfloat16), 'mp', axis=1, tiled=True)]
  transfers between devices with their start and end apart: 4 -> 3, of which waited for: 4 -> 3; matrix products, arithmetic and copies ran while one was open for 4% -> 5% of each run, Pallas kernels for 0% -> 0%
where the time goes in v1:
time: 347 us
  waiting for transfers between devices  260 us (75%)
  matrix products  34.9 us (10%)
  blocking collectives  26.3 us (8%)
  between operations  13.8 us (4%)
  other arithmetic  6.17 us (2%)
  local copies, waits for them, and re-layouts  5.86 us (2%)
    psum x1, waiting for transfers between devices, shards(): ability_sum = lax.psum(ability_partial, 'item')  126 us
    psum x1, waiting for transfers between devices, shards(): discrim_sum = lax.psum(discrim_partial, 'mp')  112 us
    all_to_all x1, blocking collectives, shards(): lax.all_to_all(jnp.stack([ability.astype(jnp.bfloat16)] * lax.axis_size('...  26.3 us
    all_gather x1, waiting for transfers between devices, shards(): lax.all_gather(discrim.astype(jnp.bfloat16), 'mp', axis=1, tiled=True)  21.6 us
    dot_general x1, matrix products, shards(): lax.dot_general(residual, ability_wide, (((0,), (0,)), ((), ())), precisi...  13.3 us
    dot_general x1, matrix products, shards(): lax.dot_general(ability_full, discrim_full, (((1,), (1,)), ((), ())), pre...  11.9 us
    dot_general x1, matrix products, shards(): ability_partial = jnp.dot(residual, discrim_wide, precision=highest)  9.74 us
  transfers between devices with their start and end apart: 3, of which 3 were waited for; matrix products, arithmetic and copies ran while one was open for 5% of the time, Pallas kernels for 0%

profile of v1, /device:TPU:8, one launch (start us, length us, event | category | flops | bytes accessed | tf_op | source)
XLA Modules:
  0.0 347.2 jit_solution(16482083117351154533)
XLA Ops:
  7.2 0.0 all-gather.2.cloned.1.call-start
  7.2 1.6 convert_element_type.12
  8.8 0.0 all-gather.2.cloned.1.call-update
  8.9 0.0 all-reduce.3.cloned.1.call-start
  8.9 0.9 convert_element_type.11
  9.8 0.1 stack.2
  9.9 26.3 %all_to_all.5 = bf16[16,2048,16]{1,2,0:T(8,128)(2,1)S(1)} all-to-all(bf16[16,2048,16]{1,2,0:T(8,128)(2,1)S(1)} %stack.2), channel_id=1, replica_groups=mesh['mp'=8,'item'=16] {'item'}, dimensions={0} | all-to-all | bytes 2097152 | tf_op jit(solution)/shard_map/all_to_all | solution.py:24
  36.2 21.6 %all-gather.2.cloned.1.call-done = bf16[2048,256]{0,1:T(8,128)(2,1)} async-done(((bf16[2048,32]{0,1:T(8,128)(2,1)}), bf16[2048,256]{0,1:T(8,128)(2,1)}) %all-gather.2.cloned.1.call-update) | async-done | bytes 1048592 | tf_op jit(solution)/shard_map/all_gather | solution.py:29
  57.8 11.9 %subtract_select_fusion = f32[2048,2048]{1,0:T(8,128)S(1)} fusion(s32[2048,2048]{1,0:T(8,128)} %param.8, bf16[2048,256]{0,1:T(8,128)(2,1)S(1)} %bitcast.9, bf16[2048,256]{0,1:T(8,128)(2,1)} %all-gather.2.cloned.1.call-done, f32[2048]{0:T(1024)} %param.9), kind=kOutput, calls=%fused_computation | convolution fusion | flops 2185232384 | bytes 35659776 | tf_op jit(solution)/shard_map/dot_general | solution.py:30
  69.7 0.0 copy-start
  69.7 5.7 %copy-done = f32[2048,2048]{1,0:T(8,128)} copy-done((f32[2048,2048]{1,0:T(8,128)}, f32[2048,2048]{1,0:T(8,128)S(1)}, u32[]{:S(2)}) %copy-start) | copy-done | bytes 16777240
  75.4 0.0 copy-done.1
  75.4 9.7 %fusion = f32[2048,256]{0,1:T(8,128)} fusion(f32[2048,2048]{1,0:T(8,128)S(1)} %subtract_select_fusion, bf16[2048,256]{0,1:T(8,128)(2,1)S(1)} %copy-done.1), kind=kOutput, calls=%fused_computation.7 | convolution fusion | flops 12884901888 | bytes 19922944 | tf_op jit(solution)/shard_map/dot_general | solution.py:43
  85.2 0.0 copy-start.4
  85.2 0.0 copy-start.5
  85.2 0.0 all-reduce.3.cloned.1.call-update
  85.2 0.2 all-reduce.5.cloned.1.call-start
  85.5 13.3 %fusion.1 = f32[2048,256]{0,1:T(8,128)} fusion(f32[2048,2048]{1,0:T(8,128)} %copy-done, bf16[2048,256]{0,1:T(8,128)(2,1)S(1)} %bitcast.10), kind=kOutput, calls=%fused_computation.8 | convolution fusion | flops 12884901888 | bytes 19922944 | tf_op jit(solution)/shard_map/dot_general | solution.py:48
  98.8 0.0 all-reduce.5.cloned.1.call-update
  98.8 126.5 %all-reduce.3.cloned.1.call-done = f32[2048,256]{0,1:T(8,128)} async-done(((f32[2048,256]{0,1:T(8,128)}), f32[2048,256]{0,1:T(8,128)}) %all-reduce.3.cloned.1.call-update) | async-done | bytes 2097168 | tf_op jit(solution)/shard_map/psum | solution.py:44
  225.3 1.7 multiply_subtract_fusion.1
  227.0 111.8 %all-reduce.5.cloned.1.call-done = f32[2048,256]{0,1:T(8,128)} async-done(((f32[2048,256]{0,1:T(8,128)}), f32[2048,256]{0,1:T(8,128)}) %all-reduce.5.cloned.1.call-update) | async-done | bytes 2097168 | tf_op jit(solution)/shard_map/psum | solution.py:51
  338.8 0.0 copy-done.2
  338.8 1.9 multiply_subtract_fusion
  (10 shorter events, 0.0 us)
Async XLA Ops:
  7.2 50.6 %all-gather.2.cloned.1.call-start = ((), (), s32[]{:S(2)}) async-start(), calls=%async_computation.1 | async-start | bytes 1179648 | tf_op jit(solution)/shard_map/all_gather | solution.py:29
  8.9 216.4 %all-reduce.3.cloned.1.call-start = ((), (), s32[]{:S(2)}) async-start(), calls=%async_computation.2 | async-start | bytes 4194304 | tf_op jit(solution)/shard_map/psum | solution.py:44
  57.8 17.6 %copy-start.1 = (bf16[2048,256]{0,1:T(8,128)(2,1)S(1)}, bf16[2048,256]{0,1:T(8,128)(2,1)}, u32[]{:S(2)}) copy-start(bf16[2048,256]{0,1:T(8,128)(2,1)} %all-gather.2.cloned.1.call-done) | copy-start | bytes 3145732
  69.7 5.7 %copy-start = (f32[2048,2048]{1,0:T(8,128)}, f32[2048,2048]{1,0:T(8,128)S(1)}, u32[]{:S(2)}) copy-start(f32[2048,2048]{1,0:T(8,128)S(1)} %subtract_select_fusion) | copy-start | bytes 50331652
  85.2 140.1 %copy-start.3 = (f32[2048,16]{0,1:T(8,128)S(1)}, f32[2048,16]{0,1:T(8,128)}, u32[]{:S(2)}) copy-start(f32[2048,16]{0,1:T(8,128)} %param.10) | copy-start | bytes 393220
  85.2 140.1 %copy-start.6 = (f32[2048,16]{0,1:T(8,128)S(1)}, f32[2048,16]{0,1:T(8,128)}, u32[]{:S(2)}) copy-start(f32[2048,16]{0,1:T(8,128)} %param.11) | copy-start | bytes 393220
  85.2 140.1 %copy-start.7 = (f32[2048,16]{0,1:T(8,128)S(1)}, f32[2048,16]{0,1:T(8,128)}, u32[]{:S(2)}) copy-start(f32[2048,16]{0,1:T(8,128)} %param.12) | copy-start | bytes 393220
  85.2 253.6 %copy-start.2 = (f32[2048,32]{0,1:T(8,128)S(1)}, f32[2048,32]{0,1:T(8,128)}, u32[]{:S(2)}) copy-start(f32[2048,32]{0,1:T(8,128)} %param.13) | copy-start | bytes 786436
  85.2 253.6 %copy-start.4 = (f32[2048,32]{0,1:T(8,128)S(1)}, f32[2048,32]{0,1:T(8,128)}, u32[]{:S(2)}) copy-start(f32[2048,32]{0,1:T(8,128)} %param.14) | copy-start | bytes 786436
  85.2 253.6 %copy-start.5 = (f32[2048,32]{0,1:T(8,128)S(1)}, f32[2048,32]{0,1:T(8,128)}, u32[]{:S(2)}) copy-start(f32[2048,32]{0,1:T(8,128)} %param.15) | copy-start | bytes 786436
  85.2 253.5 %all-reduce.5.cloned.1.call-start = ((), (), s32[]{:S(2)}) async-start(), calls=%async_computation.3 | async-start | bytes 4194304 | tf_op jit(solution)/shard_map/psum | solution.py:51
Sparse Core Ops, SparseCore 0:
  10.2 47.5 all-gather.1
  85.4 139.8 all-reduce.2
  227.8 110.9 all-reduce.4
